TPU v7x, 32 devices: a whole 2x2x4 slice. The times are simulated.
32 devices in a mesh: span: 8 (over z, x), tensor: 4 (over y, core).
Axes of the slice: x: 2, y: 2, z: 4, core: 2. Of those that a mesh axis runs over, the one named last changes fastest.
Arguments:
- latents: bfloat16 [1024, 5120], P(('span', 'tensor')), may hold values from -6 to 6
- modulation: float32 [4, 3, 5120], replicated, may hold values from -3 to 3
- w_query: bfloat16 [5120, 4096], P(None, 'tensor'), may hold values from -0.078125 to 0.078125
- w_key: bfloat16 [5120, 4096], P(None, 'tensor'), may hold values from -0.078125 to 0.078125
- w_value: bfloat16 [5120, 4096], P(None, 'tensor'), may hold values from -0.078125 to 0.078125
- w_out: bfloat16 [4096, 5120], P('tensor'), may hold values from -0.5 to 0.5
- cache_k: bfloat16 [2048, 4096], P('span', 'tensor'), may hold values from -800 to 800
- cache_v: bfloat16 [2048, 4096], P('span', 'tensor'), may hold values from -6 to 6
- level_index: int32 [8], P('span'), may hold values from 0 to 3
- rotation: int32 [8], replicated, may hold values from 0 to 7, each once
- cached_tokens: int32 [1], replicated, may hold values from 128 to 2048
Outputs:
- branch: bfloat16 [1024, 5120], P(('span', 'tensor'))
All inputs are finite; a program needn't handle non-finite values.
Results may differ from a plain program's by a relative error of at most 0.019.
Values may be sent and summed in bfloat16 or wider, within the bound.
No kernel may reach another device: no remote copies, remote signals or barrier semaphores. Data moves between devices by JAX's collectives and lax.ppermute only.
A program may use at most 128 MiB of HBM per device.

v0:
```python
import jax
import jax.numpy as jnp
from jax import lax
from jax.sharding import PartitionSpec as P

HD = 128
EPSILON = 1e-06


def block_update(running, q_heads, key_block, value_block, key_valid):
    run_max, run_sum, run_acc = running
    head_count = q_heads.shape[1]
    head_size = q_heads.shape[2]
    key_heads = key_block.reshape(key_block.shape[0], head_count, head_size)
    value_heads = value_block.reshape(value_block.shape[0], head_count, head_size)
    scores = jnp.einsum(
        "qhd,khd->hqk", q_heads, key_heads, preferred_element_type=jnp.float32
    ) * head_size ** (-0.5)
    scores = jnp.where(key_valid[None, None, :], scores, -1e30)
    new_max = jnp.maximum(run_max, jnp.max(scores, axis=-1))
    weights = jnp.where(key_valid[None, None, :], jnp.exp(scores - new_max[..., None]), 0.0)
    rescale = jnp.exp(run_max - new_max)
    run_sum = run_sum * rescale + jnp.sum(weights, axis=-1)
    run_acc = run_acc * rescale[..., None] + jnp.einsum(
        "hqk,khd->hqd",
        weights.astype(jnp.bfloat16),
        value_heads,
        preferred_element_type=jnp.float32,
    )
    return (new_max, run_sum, run_acc)


def attend(running, q_heads, key_rows, value_rows, key_valid):
    running = block_update(running, q_heads, key_rows, value_rows, key_valid)
    return running


def body(
    latents,
    modulation,
    w_query,
    w_key,
    w_value,
    w_out,
    cache_k,
    cache_v,
    level_index,
    rotation,
    cached_tokens,
):
    groups = lax.axis_size("span")
    own_index = lax.axis_index("span")
    chooser = (jnp.arange(modulation.shape[0], dtype=jnp.int32) == level_index[0]).astype(
        jnp.float32
    )
    mod_rows = jnp.sum(chooser[:, None, None] * modulation, axis=0)
    shift_row, scale_row, gate_row = (mod_rows[0], mod_rows[1], mod_rows[2])
    row_data = latents.astype(jnp.float32)
    row_mean = jnp.mean(row_data, axis=-1, keepdims=True)
    centred = row_data - row_mean
    row_var = jnp.mean(centred * centred, axis=-1, keepdims=True)
    normed = centred * lax.rsqrt(row_var + EPSILON)
    modulated = (normed * (1.0 + scale_row) + shift_row).astype(jnp.bfloat16)
    shard_piece = lax.all_gather(modulated, "tensor", axis=0, tiled=True)
    projected = [
        jnp.dot(shard_piece, weight, preferred_element_type=jnp.float32).astype(jnp.bfloat16)
        for weight in (w_query, w_key, w_value)
    ]
    joined = jnp.concatenate(projected, axis=1)
    inner_width = w_query.shape[1]
    own_query = joined[:, :inner_width]
    own_key = joined[:, inner_width : 2 * inner_width]
    own_value = joined[:, 2 * inner_width :]
    head_count = inner_width // HD
    span_rows = own_query.shape[0]
    q_heads = own_query.reshape(span_rows, head_count, HD)
    group_ids = jnp.arange(groups, dtype=jnp.int32)
    order_own = jnp.sum(jnp.where(group_ids == own_index, rotation, 0))
    live_keys = cached_tokens[0]
    initial = (
        jnp.full((head_count, span_rows), -1e30, jnp.float32),
        jnp.zeros((head_count, span_rows), jnp.float32),
        jnp.zeros((head_count, span_rows, HD), jnp.float32),
    )
    all_queries = lax.all_gather(own_query, "span", axis=0, tiled=True)
    cache_rows = cache_k.shape[0]
    local_valid = own_index * cache_rows + jnp.arange(cache_rows, dtype=jnp.int32) < live_keys

    def group_partial(group_queries):
        return attend(initial, group_queries, cache_k, cache_v, local_valid)

    partials = lax.map(group_partial, all_queries.reshape(groups, span_rows, head_count, HD))
    source_max, source_sum, source_acc = lax.all_to_all(
        partials, "span", split_axis=0, concat_axis=0, tiled=True
    )
    best_max = jnp.max(source_max, axis=0)
    rescale = jnp.exp(source_max - best_max)
    running = (
        best_max,
        jnp.sum(source_sum * rescale, axis=0),
        jnp.sum(source_acc * rescale[..., None], axis=0),
    )
    key_rows = lax.all_gather(own_key, "span", axis=0, tiled=True)
    value_rows = lax.all_gather(own_value, "span", axis=0, tiled=True)
    key_index = jnp.arange(key_rows.shape[0], dtype=jnp.int32)
    key_group = key_index // span_rows
    key_order = jnp.sum(
        jnp.where(key_group[:, None] == group_ids[None, :], rotation[None, :], 0), axis=1
    )
    key_valid = key_order <= order_own
    run_max, run_sum, run_acc = attend(running, q_heads, key_rows, value_rows, key_valid)
    attended = (
        (run_acc / run_sum[..., None])
        .transpose(1, 0, 2)
        .reshape(span_rows, inner_width)
        .astype(jnp.bfloat16)
    )
    projection = lax.psum_scatter(
        jnp.dot(attended, w_out, preferred_element_type=jnp.float32).astype(jnp.bfloat16),
        "tensor",
        scatter_dimension=0,
        tiled=True,
    ).astype(jnp.float32)
    return (gate_row[None, :] * projection).astype(jnp.bfloat16)


def solution(mesh):
    placed = (
        P(("span", "tensor"), None),
        P(),
        P(None, "tensor"),
        P(None, "tensor"),
        P(None, "tensor"),
        P("tensor", None),
        P("span", "tensor"),
        P("span", "tensor"),
        P("span"),
        P(),
        P(),
    )
    return jax.shard_map(
        body, mesh=mesh, in_specs=placed, out_specs=P(("span", "tensor"), None), check_vma=False
    )
```

profile of v0, /device:TPU:0, one launch (start us, length us, event | category | flops | bytes accessed | tf_op | source)
XLA Modules:
  0.0 317.0 jit_solution(9142673391689891589)
XLA Ops:
  10.8 1.9 fusion.49
  12.8 21.0 %all-gather.5.cloned.1.call-done = bf16[128,5120]{1,0:T(8,128)(2,1)} async-done(((bf16[32,5120]{1,0:T(8,128)(2,1)}), bf16[128,5120]{1,0:T(8,128)(2,1)}) %all-gather.5.cloned.1.call-update) | async-done | bytes 1310736 | tf_op jit(solution)/shard_map/all_gather | solution.py:64
  33.8 6.7 %convolution_convert_fusion.3 = bf16[128,1024]{1,0:T(8,128)(2,1)} fusion(bf16[128,5120]{1,0:T(8,128)(2,1)} %all-gather.5.cloned.1.call-done, bf16[5120,1024]{1,0:T(8,128)(2,1)} %param.15), kind=kOutput, calls=%fused_computation.48 | convolution fusion | flops 1342308352 | bytes 12058624 | tf_op jit(solution)/shard_map/dot_general | solution.py:66
  40.6 6.2 %convolution_convert_fusion.1 = bf16[128,1024]{1,0:T(8,128)(2,1)} fusion(bf16[128,5120]{1,0:T(8,128)(2,1)S(1)} %copy-done, bf16[5120,1024]{1,0:T(8,128)(2,1)} %param.17), kind=kOutput, calls=%fused_computation.46 | convolution fusion | flops 1342308352 | bytes 12058624 | tf_op jit(solution)/shard_map/dot_general | solution.py:66
  46.9 42.9 %all-gather.7.cloned.1.call-done = bf16[1024,1024]{1,0:T(8,128)(2,1)} async-done(((bf16[128,1024]{1,0:T(8,128)(2,1)}), bf16[1024,1024]{1,0:T(8,128)(2,1)}) %all-gather.7.cloned.1.call-update) | async-done | bytes 2097168 | tf_op jit(solution)/shard_map/all_gather | solution.py:85
  89.8 2.2 copy.38
  92.0 38.5 %while.15 = (s32[]{:T(128)}, f32[8,8,128]{2,1,0:T(8,128)S(1)}, f32[8,8,128]{2,1,0:T(8,128)S(1)}, f32[8,8,128,128]{3,2,1,0:T(8,128)}, bf16[8,128,8,128]{3,2,1,0:T...) while((s32[]{:T(128)}, f32[8,8,128]{2,1,0:T(8,128)S(1)}, ...), condition=%wide.region_6.7_spmd.clone, body=%wide.region_3.6_spmd.clone.sunk | while | flops 136713728 | bytes 5555829 | solution.py:92
  94.2 2.2 fusion.91
  97.5 1.5 fusion.88
  99.0 2.2 fusion.91
  103.8 2.2 fusion.91
  108.6 2.2 fusion.91
  111.9 1.4 fusion.88
  113.4 2.2 fusion.91
  116.7 1.5 fusion.88
  118.3 2.2 fusion.91
  123.1 2.2 fusion.91
  127.8 2.2 fusion.91
  130.5 9.8 %all_to_all.15 = f32[8,8,128]{2,1,0:T(8,128)S(1)} all-to-all(f32[8,8,128]{2,1,0:T(8,128)S(1)} %get-tuple-element.50), channel_id=1, replica_groups=mesh['span'=8,'tensor'=4] {'span'}, dimensions={0} | all-to-all | bytes 65536 | tf_op jit(solution)/shard_map/all_to_all | solution.py:93
  140.3 9.0 %all_to_all.16 = f32[8,8,128]{2,1,0:T(8,128)S(1)} all-to-all(f32[8,8,128]{2,1,0:T(8,128)S(1)} %get-tuple-element.51), channel_id=1, replica_groups=mesh['span'=8,'tensor'=4] {'span'}, dimensions={0} | all-to-all | bytes 65536 | tf_op jit(solution)/shard_map/all_to_all | solution.py:93
  149.4 4.5 %all-to-all-start = ((f32[8,8,128,128]{3,2,1,0:T(8,128)}), f32[8,8,128,128]{3,2,1,0:T(8,128)}, u32[]{:S(2)}, u32[]{:S(2)}) async-start(f32[8,8,128,128]{3,2,1,0:T(8,128)} %get-tuple-element.49), calls=%async_computation | async-start | bytes 8388608 | tf_op jit(solution)/shard_map/all_to_all | solution.py:93
  154.0 6.2 %convolution_convert_fusion.2 = bf16[128,1024]{1,0:T(8,128)(2,1)} fusion(bf16[128,5120]{1,0:T(8,128)(2,1)S(1)} %copy-done, bf16[5120,1024]{1,0:T(8,128)(2,1)} %param.16), kind=kOutput, calls=%fused_computation.47 | convolution fusion | flops 1342308352 | bytes 12058624 | tf_op jit(solution)/shard_map/dot_general | solution.py:66
  161.7 2.9 copy.32
  164.6 92.7 %all-gather.9.cloned.1.call-done = bf16[1024,1024]{1,0:T(8,128)(2,1)} async-done(((bf16[128,1024]{1,0:T(8,128)(2,1)}), bf16[1024,1024]{1,0:T(8,128)(2,1)}) %all-gather.9.cloned.1.call-update) | async-done | bytes 2097168 | tf_op jit(solution)/shard_map/all_gather | solution.py:103
  257.3 4.5 %fusion.19 = (f32[8,128]{1,0:T(8,128)S(1)}, f32[8,128,1024]{2,1,0:T(8,128)}) fusion(pred[1024]{0:T(1024)(128)(4,1)S(1)} %broadcast_compare_fusion, bf16[1024,1024]{1,0:T(8,128)(2,1)} %all-gather.9.cloned.1.call-done, bf16[128,1024]{1,0:T(8,128)(2,1)S(1)} %copy-done.1), kind=kOutput, calls=%fused_computation.32 | convolution fusion | flops 271580160 | bytes 6558720 | tf_op jit(solution)/shard_map/qhd,khd->hqk/dot_general | solution.py:16
  261.8 3.3 %fusion.20 = f32[8,128]{1,0:T(8,128)S(1)} fusion(f32[8,128,1024]{2,1,0:T(8,128)} %get-tuple-element.133, f32[8,128]{1,0:T(8,128)S(1)} %max.18, pred[1024]{0:T(1024)(128)(4,1)S(1)} %broadcast_compare_fusion), kind=kLoop, calls=%fused_computation.33 | loop fusion | flops 5241856 | bytes 4203520 | tf_op jit(solution)/shard_map/reduce_sum | solution.py:23
  265.1 4.8 %all-to-all-done = f32[8,8,128,128]{3,2,1,0:T(8,128)} async-done(((f32[8,8,128,128]{3,2,1,0:T(8,128)}), f32[8,8,128,128]{3,2,1,0:T(8,128)}, u32[]{:S(2)}, u32[]{:S(2)}) %all-to-all-start) | async-done | bytes 4194336 | tf_op jit(solution)/shard_map/all_to_all | solution.py:93
  269.9 2.9 multiply_reduce_fusion
  273.0 3.6 %fusion.41 = bf16[128,8,128]{0,2,1:T(8,128)(2,1)S(1)} fusion(bf16[1024,8,128]{0,2,1:T(8,128)(2,1)S(1)} %bitcast.117, f32[8,128,1024]{2,1,0:T(8,128)} %get-tuple-element.133, f32[8,128]{1,0:T(8,128)S(1)} %max.18, pred[1024]{0:T(1024)(128)(4,1)S(1)} %broadcast_compare_fusion, f32[8,128,128]{1,2,0:T(8,128)S(1)} %copy.28, f32[128,8]{0,1:T(8,128)S(1)} %get-tuple-element.119, ...), kind=kOutput, calls=%fused_computation.50 | convolution fusion | flops 274202624 | bytes 7091200 | tf_op jit(solution)/shard_map/hqk,khd->hqd/dot_general | solution.py:24
  276.6 6.6 %convolution_convert_fusion = bf16[128,5120]{1,0:T(8,128)(2,1)} fusion(bf16[128,1024]{0,1:T(8,128)(2,1)S(1)} %bitcast.119, bf16[1024,5120]{1,0:T(8,128)(2,1)} %param.18), kind=kOutput, calls=%fused_computation.28 | convolution fusion | flops 1342832640 | bytes 12058624 | tf_op jit(solution)/shard_map/dot_general | solution.py:119
  283.2 25.5 %reduce-scatter.2.cloned.1.call-done = bf16[32,5120]{1,0:T(8,128)(2,1)} async-done(((bf16[128,5120]{1,0:T(8,128)(2,1)}), bf16[32,5120]{1,0:T(8,128)(2,1)}) %reduce-scatter.2.cloned.1.call-update) | async-done | bytes 327696 | tf_op jit(solution)/shard_map/reduce_scatter | solution.py:118
  308.7 1.8 multiply_convert_fusion
  (81 shorter events, 21.3 us)
Async XLA Ops:
  6.5 27.3 %all-gather.5.cloned.1.call-start = ((), (), s32[]{:S(2)}) async-start(), calls=%async_computation.4 | async-start | bytes 1638400 | tf_op jit(solution)/shard_map/all_gather | solution.py:64
  12.7 77.0 %all-gather.7.cloned.1.call-start = ((), (), s32[]{:S(2)}) async-start(), calls=%async_computation.5 | async-start | bytes 2359296 | tf_op jit(solution)/shard_map/all_gather | solution.py:85
  33.8 6.8 %copy-start = (bf16[128,5120]{1,0:T(8,128)(2,1)S(1)}, bf16[128,5120]{1,0:T(8,128)(2,1)}, u32[]{:S(2)}) copy-start(bf16[128,5120]{1,0:T(8,128)(2,1)} %all-gather.5.cloned.1.call-done) | copy-start | bytes 3932164
  40.5 121.2 %all-gather.11.cloned.1.call-start = ((), (), s32[]{:S(2)}) async-start(), calls=%async_computation.7 | async-start | bytes 2359296 | tf_op jit(solution)/shard_map/all_gather | solution.py:104
  149.4 120.5 %all-to-all-start = ((f32[8,8,128,128]{3,2,1,0:T(8,128)}), f32[8,8,128,128]{3,2,1,0:T(8,128)}, u32[]{:S(2)}, u32[]{:S(2)}) async-start(f32[8,8,128,128]{3,2,1,0:T(8,128)} %get-tuple-element.49), calls=%async_computation | async-start | bytes 8388608 | tf_op jit(solution)/shard_map/all_to_all | solution.py:93
  153.9 6.6 %copy-start.2 = (s32[8]{0:T(128)S(1)}, s32[8]{0:T(128)}, u32[]{:S(2)}) copy-start(s32[8]{0:T(128)} %param.22) | copy-start | bytes 100
  153.9 103.4 %all-gather.9.cloned.1.call-start = ((), (), s32[]{:S(2)}) async-start(), calls=%async_computation.6 | async-start | bytes 2359296 | tf_op jit(solution)/shard_map/all_gather | solution.py:103
  160.2 97.1 %copy-start.1 = (bf16[128,1024]{1,0:T(8,128)(2,1)S(1)}, bf16[128,1024]{1,0:T(8,128)(2,1)}, u32[]{:S(2)}) copy-start(bf16[128,1024]{1,0:T(8,128)(2,1)} %convolution_convert_fusion.3) | copy-start | bytes 786436
  160.2 148.5 %reduce-scatter.2.cloned.1.call-start = ((), (), s32[]{:S(2)}) async-start(), calls=%async_computation.8 | async-start | bytes 1638400 | tf_op jit(solution)/shard_map/reduce_scatter | solution.py:118
Sparse Core Ops, SparseCore 0:
  12.9 20.8 all-gather.4
  40.7 49.0 all-gather.6
  91.9 48.4 all-gather.10
  160.3 96.8 all-gather.8
  283.3 25.3 reduce-scatter.1
where the time goes:
time: 319 us; the launch traced here: 317 us
  waiting for transfers between devices  187 us (59%)
  matrix products  63.2 us (20%)
  other arithmetic  23.1 us (7%)
  blocking collectives  18.9 us (6%)
  between operations  14 us (4%)
  local copies, waits for them, and re-layouts  5.46 us (2%)
  starting transfers between devices  4.89 us (2%)
    all_gather x1, waiting for transfers between devices, body(): key_rows = lax.all_gather(own_key, 'span', axis=0, tiled=True)  92.7 us
    all_gather x1, waiting for transfers between devices, body(): all_queries = lax.all_gather(own_query, 'span', axis=0, tiled=True)  42.9 us
    reduce_scatter x1, waiting for transfers between devices, body(): lax.psum_scatter(jnp.dot(attended, w_out, preferred_element_type=jnp.floa...  25.5 us
    dot_general x9, matrix products, block_update(): jnp.einsum('hqk,khd->hqd', weights.astype(jnp.bfloat16), value_heads, pre...  21.4 us
    all_gather x1, waiting for transfers between devices, body(): shard_piece = lax.all_gather(modulated, 'tensor', axis=0, tiled=True)  21 us
    dot_general x3, matrix products, body(): jnp.dot(shard_piece, weight, preferred_element_type=jnp.float32)  19.1 us
    all_to_all x2, blocking collectives, body(): lax.all_to_all(partials, 'span', split_axis=0, concat_axis=0, tiled=True)  18.9 us
    dot_general x9, matrix products, block_update(): jnp.einsum('qhd,khd->hqk', q_heads, key_heads, preferred_element_type=jnp...  16.1 us
  transfers between devices with their start and end apart: 6, of which 5 were waited for; matrix products, arithmetic and copies ran while one was open for 20% of the time, Pallas kernels for 0%

commit v1 on v0

--- a/solution.py
+++ b/solution.py
@@ -100,7 +100,9 @@
         jnp.sum(source_sum * rescale, axis=0),
         jnp.sum(source_acc * rescale[..., None], axis=0),
     )
-    key_rows = lax.all_gather(own_key, "span", axis=0, tiled=True)
+    key_rows = jnp.concatenate(
+        lax.all_to_all(jnp.stack([own_key] * lax.axis_size("span")), "span", 0, 0), axis=0
+    )
     value_rows = lax.all_gather(own_value, "span", axis=0, tiled=True)
     key_index = jnp.arange(key_rows.shape[0], dtype=jnp.int32)
     key_group = key_index // span_rows

time: 319 us -> 360 us (1.13)
  waiting for transfers between devices: 187 us -> 211 us
  local copies, waits for them, and re-layouts: 5.46 us -> 19.3 us
  starting transfers between devices: 4.89 us -> 10.4 us
    all_gather x1, waiting for transfers between devices: 0.02 us -> 93.9 us  [body(): value_rows = lax.all_gather(own_value, 'span', axis=0, tiled=True)]
    all_gather x1 -> x0, waiting for transfers between devices: 92.7 us -> none  [body(): key_rows = lax.all_gather(own_key, 'span', axis=0, tiled=True)]
    all_gather x1, waiting for transfers between devices: 42.9 us -> 68.8 us  [body(): all_queries = lax.all_gather(own_query, 'span', axis=0, tiled=True)]
    dynamic_slice x8, local copies, waits for them, and re-layouts: 0.19 us -> 7.77 us  [body(): lax.map(group_partial, all_queries.reshape(groups, span_rows, head_count,...]
    all_to_all x0 -> x1, starting transfers between devices: none -> 5.51 us  [body(): lax.all_to_all(jnp.stack([own_key] * lax.axis_size('span')), 'span', 0, 0)]
  transfers between devices with their start and end apart: 6 -> 6, of which waited for: 5 -> 5; matrix products, arithmetic and copies ran while one was open for 20% -> 21% of each run, Pallas kernels for 0% -> 0%
where the time goes in v1:
time: 360 us; the launch traced here: 358 us
  waiting for transfers between devices  211 us (59%)
  matrix products  60.8 us (17%)
  other arithmetic  23.4 us (6%)
  local copies, waits for them, and re-layouts  19.3 us (5%)
  blocking collectives  18.1 us (5%)
  between operations  14 us (4%)
  starting transfers between devices  10.4 us (3%)
    all_gather x1, waiting for transfers between devices, body(): value_rows = lax.all_gather(own_value, 'span', axis=0, tiled=True)  93.9 us
    all_gather x1, waiting for transfers between devices, body(): all_queries = lax.all_gather(own_query, 'span', axis=0, tiled=True)  68.8 us
    reduce_scatter x1, waiting for transfers between devices, body(): lax.psum_scatter(jnp.dot(attended, w_out, preferred_element_type=jnp.floa...  25.2 us
    dot_general x9, matrix products, block_update(): jnp.einsum('hqk,khd->hqd', weights.astype(jnp.bfloat16), value_heads, pre...  21.4 us
    all_gather x1, waiting for transfers between devices, body(): shard_piece = lax.all_gather(modulated, 'tensor', axis=0, tiled=True)  21 us
    dot_general x3, matrix products, body(): jnp.dot(shard_piece, weight, preferred_element_type=jnp.float32)  18.4 us
    all_to_all x2, blocking collectives, body(): lax.all_to_all(partials, 'span', split_axis=0, concat_axis=0, tiled=True)  18.1 us
    dot_general x9, matrix products, block_update(): jnp.einsum('qhd,khd->hqk', q_heads, key_heads, preferred_element_type=jnp...  14.4 us
  transfers between devices with their start and end apart: 6, of which 5 were waited for; matrix products, arithmetic and copies ran while one was open for 21% of the time, Pallas kernels for 0%

profile of v1, /device:TPU:0, one launch (start us, length us, event | category | flops | bytes accessed | tf_op | source)
XLA Modules:
  0.0 357.7 jit_solution(4951630534873161786)
XLA Ops:
  10.8 1.9 fusion.48
  12.8 21.0 %all-gather.4.cloned.1.call-done = bf16[128,5120]{1,0:T(8,128)(2,1)} async-done(((bf16[32,5120]{1,0:T(8,128)(2,1)}), bf16[128,5120]{1,0:T(8,128)(2,1)}) %all-gather.4.cloned.1.call-update) | async-done | bytes 1310736 | tf_op jit(solution)/shard_map/all_gather | solution.py:64
  33.8 6.7 %convolution_convert_fusion.3 = bf16[128,1024]{1,0:T(8,128)(2,1)} fusion(bf16[128,5120]{1,0:T(8,128)(2,1)} %all-gather.4.cloned.1.call-done, bf16[5120,1024]{1,0:T(8,128)(2,1)} %param.15), kind=kOutput, calls=%fused_computation.47 | convolution fusion | flops 1342308352 | bytes 12058624 | tf_op jit(solution)/shard_map/dot_general | solution.py:66
  40.6 5.5 %convolution_convert_fusion.2 = bf16[128,1024]{1,0:T(8,128)(2,1)S(1)} fusion(bf16[128,5120]{1,0:T(8,128)(2,1)S(1)} %copy-done, bf16[5120,1024]{1,0:T(8,128)(2,1)} %param.16), kind=kOutput, calls=%fused_computation.46 | convolution fusion | flops 1342308352 | bytes 12058624 | tf_op jit(solution)/shard_map/dot_general | solution.py:66
  46.1 1.6 stack.2
  47.7 5.5 %all-to-all-start.2 = ((bf16[8,128,1024]{2,1,0:T(8,128)(2,1)}), bf16[8,128,1024]{2,1,0:T(8,128)(2,1)S(1)}, u32[]{:S(2)}, u32[]{:S(2)}) async-start(bf16[8,128,1024]{2,1,0:T(8,128)(2,1)} %stack.2), calls=%async_computation.2 | async-start | bytes 4194304 | tf_op jit(solution)/shard_map/all_to_all | solution.py:104
  53.2 68.8 %all-gather.6.cloned.1.call-done = bf16[1024,1024]{1,0:T(8,128)(2,1)} async-done(((bf16[128,1024]{1,0:T(8,128)(2,1)}), bf16[1024,1024]{1,0:T(8,128)(2,1)}) %all-gather.6.cloned.1.call-update) | async-done | bytes 2097168 | tf_op jit(solution)/shard_map/all_gather | solution.py:85
  122.0 3.5 copy.42
  125.6 45.9 %while.15 = (s32[]{:T(128)}, f32[8,8,128]{2,1,0:T(8,128)S(1)}, f32[8,8,128]{2,1,0:T(8,128)S(1)}, f32[8,8,128,128]{3,2,1,0:T(8,128)}, bf16[8,128,8,128]{3,2,1,0:T...) while((s32[]{:T(128)}, f32[8,8,128]{2,1,0:T(8,128)S(1)}, ...), condition=%wide.region_6.7_spmd.clone, body=%wide.region_3.6_spmd.clone.sunk | while | flops 136713728 | bytes 5555829 | solution.py:92
  128.7 2.2 fusion.89
  134.4 2.2 fusion.89
  140.1 2.2 fusion.89
  145.9 2.2 fusion.89
  151.6 2.2 fusion.89
  157.3 2.2 fusion.89
  163.1 2.2 fusion.89
  168.8 2.2 fusion.89
  171.5 9.1 %all_to_all.20 = f32[8,8,128]{2,1,0:T(8,128)S(1)} all-to-all(f32[8,8,128]{2,1,0:T(8,128)S(1)} %get-tuple-element.50), channel_id=1, replica_groups=mesh['span'=8,'tensor'=4] {'span'}, dimensions={0} | all-to-all | bytes 65536 | tf_op jit(solution)/shard_map/all_to_all | solution.py:93
  180.5 9.0 %all_to_all.21 = f32[8,8,128]{2,1,0:T(8,128)S(1)} all-to-all(f32[8,8,128]{2,1,0:T(8,128)S(1)} %get-tuple-element.51), channel_id=1, replica_groups=mesh['span'=8,'tensor'=4] {'span'}, dimensions={0} | all-to-all | bytes 65536 | tf_op jit(solution)/shard_map/all_to_all | solution.py:93
  189.6 4.5 %all-to-all-start = ((f32[8,8,128,128]{3,2,1,0:T(8,128)}), f32[8,8,128,128]{3,2,1,0:T(8,128)}, u32[]{:S(2)}, u32[]{:S(2)}) async-start(f32[8,8,128,128]{3,2,1,0:T(8,128)} %get-tuple-element.49), calls=%async_computation | async-start | bytes 8388608 | tf_op jit(solution)/shard_map/all_to_all | solution.py:93
  194.2 6.2 %convolution_convert_fusion.1 = bf16[128,1024]{1,0:T(8,128)(2,1)} fusion(bf16[128,5120]{1,0:T(8,128)(2,1)S(1)} %copy-done, bf16[5120,1024]{1,0:T(8,128)(2,1)} %param.17), kind=kOutput, calls=%fused_computation.45 | convolution fusion | flops 1342308352 | bytes 12058624 | tf_op jit(solution)/shard_map/dot_general | solution.py:66
  202.1 2.2 copy.43
  204.3 93.9 %all-gather.8.cloned.1.call-done = bf16[1024,1024]{1,0:T(8,128)(2,1)} async-done(((bf16[128,1024]{1,0:T(8,128)(2,1)}), bf16[1024,1024]{1,0:T(8,128)(2,1)}) %all-gather.8.cloned.1.call-update) | async-done | bytes 2097168 | tf_op jit(solution)/shard_map/all_gather | solution.py:106
  298.2 3.9 %copy.37 = bf16[1024,1024]{0,1:T(8,128)(2,1)} copy(bf16[1024,1024]{1,0:T(8,128)(2,1)} %all-gather.8.cloned.1.call-done) | data formatting | bytes 4194304 | tf_op jit(solution)/shard_map/reshape | solution.py:15
  302.2 2.9 fusion.19
  305.1 3.5 fusion.20
  308.6 2.3 all-to-all-done
  310.8 2.9 multiply_reduce_fusion
  313.9 3.6 fusion.40
  317.5 6.6 %convolution_convert_fusion = bf16[128,5120]{1,0:T(8,128)(2,1)} fusion(bf16[128,1024]{0,1:T(8,128)(2,1)S(1)} %bitcast.115, bf16[1024,5120]{1,0:T(8,128)(2,1)} %param.18), kind=kOutput, calls=%fused_computation.28 | convolution fusion | flops 1342832640 | bytes 12058624 | tf_op jit(solution)/shard_map/dot_general | solution.py:121
  324.2 25.2 %reduce-scatter.2.cloned.1.call-done = bf16[32,5120]{1,0:T(8,128)(2,1)} async-done(((bf16[128,5120]{1,0:T(8,128)(2,1)}), bf16[32,5120]{1,0:T(8,128)(2,1)}) %reduce-scatter.2.cloned.1.call-update) | async-done | bytes 327696 | tf_op jit(solution)/shard_map/reduce_scatter | solution.py:120
  349.4 1.8 multiply_convert_fusion
  (86 shorter events, 33.3 us)
Async XLA Ops:
  6.5 27.3 %all-gather.4.cloned.1.call-start = ((), (), s32[]{:S(2)}) async-start(), calls=%async_computation.5 | async-start | bytes 1638400 | tf_op jit(solution)/shard_map/all_gather | solution.py:64
  12.7 109.3 %all-gather.6.cloned.1.call-start = ((), (), s32[]{:S(2)}) async-start(), calls=%async_computation.6 | async-start | bytes 2359296 | tf_op jit(solution)/shard_map/all_gather | solution.py:85
  33.8 6.8 %copy-start = (bf16[128,5120]{1,0:T(8,128)(2,1)S(1)}, bf16[128,5120]{1,0:T(8,128)(2,1)}, u32[]{:S(2)}) copy-start(bf16[128,5120]{1,0:T(8,128)(2,1)} %all-gather.4.cloned.1.call-done) | copy-start | bytes 3932164
  47.7 123.8 %all-to-all-start.2 = ((bf16[8,128,1024]{2,1,0:T(8,128)(2,1)}), bf16[8,128,1024]{2,1,0:T(8,128)(2,1)S(1)}, u32[]{:S(2)}, u32[]{:S(2)}) async-start(bf16[8,128,1024]{2,1,0:T(8,128)(2,1)} %stack.2), calls=%async_computation.2 | async-start | bytes 4194304 | tf_op jit(solution)/shard_map/all_to_all | solution.py:104
  171.5 18.1 %copy-start.1 = (bf16[8,128,1024]{2,1,0:T(8,128)(2,1)}, bf16[8,128,1024]{2,1,0:T(8,128)(2,1)S(1)}, u32[]{:S(2)}) copy-start(bf16[8,128,1024]{2,1,0:T(8,128)(2,1)S(1)} %all-to-all-done.2) | copy-start | bytes 6291460
  189.6 121.3 %all-to-all-start = ((f32[8,8,128,128]{3,2,1,0:T(8,128)}), f32[8,8,128,128]{3,2,1,0:T(8,128)}, u32[]{:S(2)}, u32[]{:S(2)}) async-start(f32[8,8,128,128]{3,2,1,0:T(8,128)} %get-tuple-element.49), calls=%async_computation | async-start | bytes 8388608 | tf_op jit(solution)/shard_map/all_to_all | solution.py:93
  194.1 6.5 %copy-start.4 = (s32[8]{0:T(128)S(1)}, s32[8]{0:T(128)}, u32[]{:S(2)}) copy-start(s32[8]{0:T(128)} %param.22) | copy-start | bytes 100
  194.2 104.1 %all-gather.8.cloned.1.call-start = ((), (), s32[]{:S(2)}) async-start(), calls=%async_computation.7 | async-start | bytes 2359296 | tf_op jit(solution)/shard_map/all_gather | solution.py:106
  200.4 148.9 %reduce-scatter.2.cloned.1.call-start = ((), (), s32[]{:S(2)}) async-start(), calls=%async_computation.8 | async-start | bytes 1638400 | tf_op jit(solution)/shard_map/reduce_scatter | solution.py:120
  202.0 100.1 %copy-start.2 = (bf16[128,1024]{1,0:T(8,128)(2,1)S(1)}, bf16[128,1024]{1,0:T(8,128)(2,1)}, u32[]{:S(2)}) copy-start(bf16[128,1024]{1,0:T(8,128)(2,1)} %convolution_convert_fusion.3) | copy-start | bytes 786436
  305.1 8.8 %copy-start.3 = (bf16[1024,1024]{0,1:T(8,128)(2,1)S(1)}, bf16[1024,1024]{0,1:T(8,128)(2,1)}, u32[]{:S(2)}) copy-start(bf16[1024,1024]{0,1:T(8,128)(2,1)} %copy.37) | copy-start | bytes 6291460
Sparse Core Ops, SparseCore 0:
  12.9 20.8 all-gather.3
  40.6 81.3 all-gather.5
  200.6 97.6 all-gather.7
  324.3 25.0 reduce-scatter.1
